TPU v7x, 128 devices: a whole 4x4x4 slice. The times are simulated.
128 devices in a mesh: frames: 4 (over z_lo, core), rows: 32 (over z_hi, y, x).
Axes of the slice: x: 4, y: 4, z: 4 (z_hi: 2, z_lo: 2; z = z_hi * 2 + z_lo), core: 2. Of those that a mesh axis runs over, the one named last changes fastest.
Arguments:
- clip_in: bfloat16 [16, 128, 64, 256], P('frames', 'rows'), may hold values from -6 to 6
- kernel_one: bfloat16 [3, 3, 3, 64, 64], replicated, may hold values from -0.15625 to 0.15625
- bias_one: float32 [64], replicated, may hold values from -3 to 3
- kernel_two: bfloat16 [3, 3, 3, 64, 64], replicated, may hold values from -0.3125 to 0.3125
- cotangent: bfloat16 [16, 128, 64, 256], P('frames', 'rows'), may hold values from -6 to 6
Outputs:
- block_out: bfloat16 [16, 128, 64, 256], P('frames', 'rows')
- grad_input: bfloat16 [16, 128, 64, 256], P('frames', 'rows')
- grad_first: float32 [3, 3, 3, 64, 64], replicated
- grad_second: float32 [3, 3, 3, 64, 64], replicated
- grad_bias: float32 [64], replicated
All inputs are finite; a program needn't handle non-finite values.
Results may differ from a plain program's by a relative error of at most 0.0065.
Values may be sent and summed in bfloat16 or wider, within the bound.
No kernel may reach another device: no remote copies, remote signals or barrier semaphores. Data moves between devices by JAX's collectives and lax.ppermute only.
A program may use at most 64 MiB of HBM per device.

v0:
```python
import math
import jax
import jax.numpy as jnp
from jax import lax
from jax.sharding import PartitionSpec as P


def with_halo(block, sides, width):
    for axis, dim in sides:
        count = lax.axis_size(axis)
        forward = [(i, i + 1) for i in range(count - 1)]
        backward = [(target, source) for source, target in forward]
        low = lax.ppermute(
            lax.slice_in_dim(block, block.shape[dim] - width, None, axis=dim), axis, forward
        )
        high = lax.ppermute(lax.slice_in_dim(block, 0, width, axis=dim), axis, backward)
        block = jnp.concatenate([low, block, high], axis=dim)
    return block


def passed_along(value, axis, by):
    devices = lax.axis_size(axis)
    pairs = [(i, i + by) for i in range(devices) if 0 <= i + by < devices]
    return lax.ppermute(value, axis, pairs)


def extend_rows(field):
    return with_halo(field, (("rows", 1),), 1)


def with_prior(field):
    earlier = passed_along(field[-2:], "frames", 1)
    return jnp.concatenate([earlier, field], axis=0)


def with_later(field):
    following = passed_along(field[:2], "frames", -1)
    return jnp.concatenate([field, following], axis=0)


def spatial_taps(extended, row_count, col_count, flipped):
    padded = jnp.pad(extended, ((0, 0), (0, 0), (0, 0), (1, 1)))
    pieces = []
    for i in range(3):
        for j in range(3):
            row_start = 2 - i if flipped else i
            col_start = 2 - j if flipped else j
            pieces.append(
                padded[:, row_start : row_start + row_count, :, col_start : col_start + col_count]
            )
    return jnp.concatenate(pieces, axis=2)


def forward_conv(extended, kernel, frame_count, row_count, col_count):
    taps = spatial_taps(extended, row_count, col_count, False)
    chan_out = kernel.shape[3]
    running = None
    for t in range(3):
        flat_kernel = jnp.transpose(kernel[t], (2, 0, 1, 3)).reshape((chan_out, -1))
        term = jnp.einsum(
            "ok,frkw->frow",
            flat_kernel,
            taps[t : t + frame_count],
            preferred_element_type=jnp.float32,
        )
        running = term if running is None else running + term
    return running


def adjoint_conv(extended, kernel, frame_count, row_count, col_count):
    taps = spatial_taps(extended, row_count, col_count, True)
    chan_in = kernel.shape[4]
    running = None
    for t in range(3):
        flat_kernel = jnp.transpose(kernel[t], (3, 0, 1, 2)).reshape((chan_in, -1))
        term = jnp.einsum(
            "ck,frkw->frcw",
            flat_kernel,
            taps[2 - t : 2 - t + frame_count],
            preferred_element_type=jnp.float32,
        )
        running = term if running is None else running + term
    return running


def kernel_grad(upstream, extended):
    frame_count, row_count, chan_out, col_count = upstream.shape
    chan_in = extended.shape[2]
    taps = spatial_taps(extended, row_count, col_count, False)
    pieces = []
    for t in range(3):
        flat = jnp.einsum(
            "frow,frkw->ok", upstream, taps[t : t + frame_count], preferred_element_type=jnp.float32
        )
        pieces.append(jnp.transpose(flat.reshape((chan_out, 3, 3, chan_in)), (1, 2, 0, 3)))
    return jnp.stack(pieces, axis=0)


def per_device(clip_in, kernel_one, bias_one, kernel_two, cotangent):
    frame_count, row_count, channels, col_count = clip_in.shape
    input_rows = extend_rows(clip_in)
    cot_rows = None
    input_ext = with_prior(input_rows)
    hidden = (
        forward_conv(input_ext, kernel_one, frame_count, row_count, col_count)
        + bias_one[None, None, :, None]
    )
    active = jax.nn.silu(hidden).astype(jnp.bfloat16)
    active_ext = with_prior(extend_rows(active))
    block_out = (
        clip_in.astype(jnp.float32)
        + forward_conv(active_ext, kernel_two, frame_count, row_count, col_count)
    ).astype(jnp.bfloat16)
    cot_rows = extend_rows(cotangent)
    cot_ext = with_later(cot_rows)
    grad_act = adjoint_conv(cot_ext, kernel_two, frame_count, row_count, col_count)
    sig = jax.nn.sigmoid(hidden)
    grad_pre = (grad_act * sig * (1.0 + hidden * (1.0 - sig))).astype(jnp.bfloat16)
    pre_ext = with_later(extend_rows(grad_pre))
    grad_back = adjoint_conv(pre_ext, kernel_one, frame_count, row_count, col_count)
    grad_input = (cotangent.astype(jnp.float32) + grad_back).astype(jnp.bfloat16)
    term_second = kernel_grad(cotangent, active_ext)
    term_first = kernel_grad(grad_pre, input_ext)
    term_bias = jnp.sum(grad_pre.astype(jnp.float32), axis=(0, 1, 3))
    total_first, total_second, total_bias = lax.psum(
        (term_first, term_second, term_bias), ("frames", "rows")
    )
    cell_total = (
        frame_count * lax.axis_size("frames") * row_count * lax.axis_size("rows") * col_count
    )
    inv_scale = 1.0 / math.sqrt(cell_total)
    return (
        block_out,
        grad_input,
        total_first * inv_scale,
        total_second * inv_scale,
        total_bias * inv_scale,
    )


def solution(mesh):
    in_specs = (P("frames", "rows", None, None), P(), P(), P(), P("frames", "rows", None, None))
    out_specs = (P("frames", "rows", None, None), P("frames", "rows", None, None), P(), P(), P())
    return jax.shard_map(
        per_device, mesh=mesh, in_specs=in_specs, out_specs=out_specs, check_vma=False
    )
```

profile of v0, /device:TPU:1, one launch (start us, length us, event | category | flops | bytes accessed | tf_op | source)
XLA Modules:
  0.0 345.2 jit_solution(11832718589891835297)
XLA Ops:
  7.2 1.7 fusion.59
  9.0 1.3 collective-permute-start.1
  10.2 5.2 %collective-permute-start = (bf16[4,1,64,256]{3,2,1,0:T(8,128)(2,1)}, bf16[4,1,64,256]{3,2,1,0:T(8,128)(2,1)}, u32[]{:S(2)}, u32[]{:S(2)}) collective-permute-start(bf16[4,1,64,256]{3,2,1,0:T(8,128)(2,1)} %get-tuple-element.19), channel_id=1, source_target_pairs={{0,1},{1,2},{2,3},{3,4},{4,5},{5,6},{6,7},{7,8},{8,9},{9,10},{10,1... | collective-permute-start | bytes 393224 | tf_op jit(solution)/shard_map/ppermute | solution.py:13
  15.5 1.0 fusion.57
  16.5 1.3 collective-permute-start.7
  17.8 4.0 %collective-permute-start.6 = (bf16[4,1,64,256]{3,2,1,0:T(8,128)(2,1)S(1)}, bf16[4,1,64,256]{3,2,1,0:T(8,128)(2,1)S(1)}, u32[]{:S(2)}, u32[]{:S(2)}) collective-permute-start(bf16[4,1,64,256]{3,2,1,0:T(8,128)(2,1)S(1)} %get-tuple-element.15), channel_id=1, source_target_pairs={{0,1},{1,2},{2,3},{3,4},{4,5},{5,6},{6,7},{7,8},{8,9},{9,10},{10,1... | collective-permute-start | bytes 393224 | tf_op jit(solution)/shard_map/ppermute | solution.py:13
  21.8 2.0 fusion.60
  23.7 1.1 constant_dynamic-update-slice_fusion.4
  24.9 4.4 %collective-permute-start.8 = (bf16[2,6,64,256]{3,2,1,0:T(8,128)(2,1)S(1)}, bf16[2,6,64,256]{3,2,1,0:T(8,128)(2,1)S(1)}, u32[]{:S(2)}, u32[]{:S(2)}) collective-permute-start(bf16[2,6,64,256]{3,2,1,0:T(8,128)(2,1)S(1)} %slice.318), channel_id=1, source_target_pairs={{32,0},{64,32},{96,64},{33,1},{65,33},{97,65},{34,2},{66,34},{98,6... | collective-permute-start | bytes 1179656 | tf_op jit(solution)/shard_map/ppermute | solution.py:24
  29.3 1.9 fusion.61
  31.2 0.8 copy.28
  32.6 0.8 copy.38
  33.4 0.9 constant_dynamic-update-slice_fusion.2
  34.4 3.6 %collective-permute-start.2 = (bf16[2,6,64,256]{3,2,1,0:T(8,128)(2,1)S(1)}, bf16[2,6,64,256]{3,2,1,0:T(8,128)(2,1)S(1)}, u32[]{:S(2)}, u32[]{:S(2)}) collective-permute-start(bf16[2,6,64,256]{3,2,1,0:T(8,128)(2,1)S(1)} %slice.306), channel_id=1, source_target_pairs={{0,32},{32,64},{64,96},{1,33},{33,65},{65,97},{2,34},{34,66},{66,9... | collective-permute-start | bytes 1179656 | tf_op jit(solution)/shard_map/ppermute | solution.py:24
  40.3 1.0 fusion.66
  41.3 1.0 fusion.65
  42.4 2.6 collective-permute-done.2
  47.3 1.1 fusion.63
  48.4 1.0 fusion.62
  49.5 1.3 multiply_convert_fusion
  50.7 1.5 convert_reduce_fusion
  52.2 1.4 fusion
  53.6 2.1 fusion.2
  55.7 2.1 fusion.4
  57.8 1.8 collective-permute-start.3
  59.6 1.3 collective-permute-start.4
  61.0 4.0 %collective-permute-start.9 = (bf16[4,1,64,256]{3,2,1,0:T(8,128)(2,1)S(1)}, bf16[4,1,64,256]{3,2,1,0:T(8,128)(2,1)S(1)}, u32[]{:S(2)}, u32[]{:S(2)}) collective-permute-start(bf16[4,1,64,256]{3,2,1,0:T(8,128)(2,1)S(1)} %get-tuple-element.12), channel_id=1, source_target_pairs={{0,1},{1,2},{2,3},{3,4},{4,5},{5,6},{6,7},{7,8},{8,9},{9,10},{10,1... | collective-permute-start | bytes 393224 | tf_op jit(solution)/shard_map/ppermute | solution.py:13
  65.0 1.3 collective-permute-start.10
  66.3 92.7 %psum.23 = f32[64]{0:T(128)S(1)} all-reduce(f32[64]{0:T(128)S(1)} %get-tuple-element.34), channel_id=1, replica_groups=mesh['frames'=4,'rows'=32] {'frames','rows'}, use_global_device_ids=true, to_apply=%region_3.4 | all-reduce | flops 64 | bytes 512 | tf_op jit(solution)/shard_map/psum | solution.py:125
  159.0 3.9 %collective-permute-start.5 = (bf16[2,6,64,256]{3,2,1,0:T(8,128)(2,1)S(1)}, bf16[2,6,64,256]{3,2,1,0:T(8,128)(2,1)S(1)}, u32[]{:S(2)}, u32[]{:S(2)}) collective-permute-start(bf16[2,6,64,256]{3,2,1,0:T(8,128)(2,1)S(1)} %pad_maximum_fusion.7), channel_id=1, source_target_pairs={{0,32},{32,64},{64,96},{1,33},{33,65},{65,97},{2,34},{34,66},{66,9... | collective-permute-start | bytes 1179656 | tf_op jit(solution)/shard_map/ppermute | solution.py:24
  163.5 2.1 pad_maximum_fusion.3
  165.6 0.8 pad_maximum_fusion.5
  166.4 2.1 collective-permute-start.11
  170.9 1.5 convolution_bitcast_fusion
  172.4 1.5 convolution_bitcast_fusion.1
  173.9 1.5 convolution_bitcast_fusion.2
  175.9 4.4 %fusion.64 = f32[4,4,256,64]{2,3,1,0:T(8,128)} fusion(bf16[6,4,576,256]{3,2,1,0:T(8,128)(2,1)} %copy-done, bf16[64,576,1,1]{0,1,3,2:T(8,128)(2,1)S(1)} %bitcast.194), kind=kOutput, calls=%fused_computation.143 | convolution fusion | flops 301989888 | bytes 8200192 | tf_op jit(solution)/shard_map/ok,frkw->frow/dot_general | solution.py:60
  182.6 2.9 copy-done.1
  185.5 1.0 pad_maximum_fusion.4
  186.6 3.9 %convolution_add_fusion.4 = f32[4,4,256,64]{2,3,1,0:T(8,128)S(1)} fusion(f32[4,4,256,64]{2,3,1,0:T(8,128)} %fusion.64, bf16[6,4,576,256]{3,2,1,0:T(8,128)(2,1)} %copy-done, bf16[64,576,1,1]{0,1,3,2:T(8,128)(2,1)S(1)} %bitcast.192), kind=kOutput, calls=%fused_computation.44 | convolution fusion | flops 302252032 | bytes 9248768 | tf_op jit(solution)/shard_map/ok,frkw->frow/dot_general | solution.py:60
  190.4 4.5 %fusion.19 = bf16[4,4,64,256]{3,2,1,0:T(8,128)(2,1)} fusion(f32[4,4,256,64]{2,3,1,0:T(8,128)S(1)} %convolution_add_fusion.4, bf16[6,4,576,256]{3,2,1,0:T(8,128)(2,1)} %copy-done, bf16[64,576,1,1]{0,1,3,2:T(8,128)(2,1)} %bitcast.193, bf16[4,4,64,256]{3,2,1,0:T(8,128)(2,1)S(1)} %copy-done.4), kind=kOutput, calls=%fused_computation.63 | convolution fusion | flops 303038464 | bytes 9248768 | tf_op jit(solution)/shard_map/ok,frkw->frow/dot_general | solution.py:60
  195.0 1.1 fusion.67
  196.0 1.1 convolution_add_fusion.1
  197.1 1.9 fusion.17
  199.0 135.3 %all-reduce.7.cloned.1.call-done = (f32[3,3,3,64,64]{3,4,2,1,0:T(8,128)}, f32[3,3,3,64,64]{3,4,2,1,0:T(8,128)}) async-done(((f32[3,3,3,64,64]{3,4,2,1,0:T(8,128)}, f32[3,3,3,64,64]{3,4,2,1,0:T(8,128)}), (f32[3,3,3,64,64]{3,4,2,1,0:T(8,128)}, f32[3,3,3,64,64]{3,4,2,1,0:T(8,128)})) %all-reduce.7.cloned.1.call-update) | async-done | bytes 884752 | tf_op jit(solution)/shard_map/psum | solution.py:125
  334.3 1.6 broadcast_multiply_fusion
  335.9 1.2 copy.53
  337.1 1.2 copy.52
  (96 shorter events, 11.0 us)
Async XLA Ops:
  7.2 27.2 %copy-start.3 = (bf16[4,4,64,256]{3,2,1,0:T(8,128)(2,1)S(1)}, bf16[4,4,64,256]{3,2,1,0:T(8,128)(2,1)}, u32[]{:S(2)}) copy-start(bf16[4,4,64,256]{3,2,1,0:T(8,128)(2,1)} %param.5) | copy-start | bytes 1572868
  7.2 327.1 %all-reduce.7.cloned.1.call-start = ((), (), s32[]{:S(2)}) async-start(), calls=%async_computation | async-start | bytes 3538944 | tf_op jit(solution)/shard_map/psum | solution.py:125
  9.0 25.4 %collective-permute-start.1 = (bf16[4,1,64,256]{3,2,1,0:T(8,128)(2,1)}, bf16[4,1,64,256]{3,2,1,0:T(8,128)(2,1)S(1)}, u32[]{:S(2)}, u32[]{:S(2)}) collective-permute-start(bf16[4,1,64,256]{3,2,1,0:T(8,128)(2,1)} %get-tuple-element.18), channel_id=1, source_target_pairs={{1,0},{2,1},{3,2},{4,3},{5,4},{6,5},{7,6},{8,7},{9,8},{10,9},{11,1... | collective-permute-start | bytes 393224 | tf_op jit(solution)/shard_map/ppermute | solution.py:16
  10.2 23.2 %collective-permute-start = (bf16[4,1,64,256]{3,2,1,0:T(8,128)(2,1)}, bf16[4,1,64,256]{3,2,1,0:T(8,128)(2,1)}, u32[]{:S(2)}, u32[]{:S(2)}) collective-permute-start(bf16[4,1,64,256]{3,2,1,0:T(8,128)(2,1)} %get-tuple-element.19), channel_id=1, source_target_pairs={{0,1},{1,2},{2,3},{3,4},{4,5},{5,6},{6,7},{7,8},{8,9},{9,10},{10,1... | collective-permute-start | bytes 393224 | tf_op jit(solution)/shard_map/ppermute | solution.py:13
  16.5 8.4 %collective-permute-start.7 = (bf16[4,1,64,256]{3,2,1,0:T(8,128)(2,1)S(1)}, bf16[4,1,64,256]{3,2,1,0:T(8,128)(2,1)S(1)}, u32[]{:S(2)}, u32[]{:S(2)}) collective-permute-start(bf16[4,1,64,256]{3,2,1,0:T(8,128)(2,1)S(1)} %get-tuple-element.14), channel_id=1, source_target_pairs={{1,0},{2,1},{3,2},{4,3},{5,4},{6,5},{7,6},{8,7},{9,8},{10,9},{11,1... | collective-permute-start | bytes 393224 | tf_op jit(solution)/shard_map/ppermute | solution.py:16
  17.8 6.0 %collective-permute-start.6 = (bf16[4,1,64,256]{3,2,1,0:T(8,128)(2,1)S(1)}, bf16[4,1,64,256]{3,2,1,0:T(8,128)(2,1)S(1)}, u32[]{:S(2)}, u32[]{:S(2)}) collective-permute-start(bf16[4,1,64,256]{3,2,1,0:T(8,128)(2,1)S(1)} %get-tuple-element.15), channel_id=1, source_target_pairs={{0,1},{1,2},{2,3},{3,4},{4,5},{5,6},{6,7},{7,8},{8,9},{9,10},{10,1... | collective-permute-start | bytes 393224 | tf_op jit(solution)/shard_map/ppermute | solution.py:13
  24.9 13.1 %collective-permute-start.8 = (bf16[2,6,64,256]{3,2,1,0:T(8,128)(2,1)S(1)}, bf16[2,6,64,256]{3,2,1,0:T(8,128)(2,1)S(1)}, u32[]{:S(2)}, u32[]{:S(2)}) collective-permute-start(bf16[2,6,64,256]{3,2,1,0:T(8,128)(2,1)S(1)} %slice.318), channel_id=1, source_target_pairs={{32,0},{64,32},{96,64},{33,1},{65,33},{97,65},{34,2},{66,34},{98,6... | collective-permute-start | bytes 1179656 | tf_op jit(solution)/shard_map/ppermute | solution.py:24
  34.4 10.5 %collective-permute-start.2 = (bf16[2,6,64,256]{3,2,1,0:T(8,128)(2,1)S(1)}, bf16[2,6,64,256]{3,2,1,0:T(8,128)(2,1)S(1)}, u32[]{:S(2)}, u32[]{:S(2)}) collective-permute-start(bf16[2,6,64,256]{3,2,1,0:T(8,128)(2,1)S(1)} %slice.306), channel_id=1, source_target_pairs={{0,32},{32,64},{64,96},{1,33},{33,65},{65,97},{2,34},{34,66},{66,9... | collective-permute-start | bytes 1179656 | tf_op jit(solution)/shard_map/ppermute | solution.py:24
  46.9 2.5 copy-start.8
  47.0 2.5 copy-start.10
  48.4 2.4 copy-start.9
  57.8 101.2 %collective-permute-start.3 = (bf16[4,1,64,256]{3,2,1,0:T(8,128)(2,1)S(1)}, bf16[4,1,64,256]{3,2,1,0:T(8,128)(2,1)S(1)}, u32[]{:S(2)}, u32[]{:S(2)}) collective-permute-start(bf16[4,1,64,256]{3,2,1,0:T(8,128)(2,1)S(1)} %get-tuple-element.16), channel_id=1, source_target_pairs={{0,1},{1,2},{2,3},{3,4},{4,5},{5,6},{6,7},{7,8},{8,9},{9,10},{10,1... | collective-permute-start | bytes 393224 | tf_op jit(solution)/shard_map/ppermute | solution.py:13
  59.6 99.3 %collective-permute-start.4 = (bf16[4,1,64,256]{3,2,1,0:T(8,128)(2,1)S(1)}, bf16[4,1,64,256]{3,2,1,0:T(8,128)(2,1)S(1)}, u32[]{:S(2)}, u32[]{:S(2)}) collective-permute-start(bf16[4,1,64,256]{3,2,1,0:T(8,128)(2,1)S(1)} %get-tuple-element.17), channel_id=1, source_target_pairs={{1,0},{2,1},{3,2},{4,3},{5,4},{6,5},{7,6},{8,7},{9,8},{10,9},{11,1... | collective-permute-start | bytes 393224 | tf_op jit(solution)/shard_map/ppermute | solution.py:16
  61.0 104.6 %collective-permute-start.9 = (bf16[4,1,64,256]{3,2,1,0:T(8,128)(2,1)S(1)}, bf16[4,1,64,256]{3,2,1,0:T(8,128)(2,1)S(1)}, u32[]{:S(2)}, u32[]{:S(2)}) collective-permute-start(bf16[4,1,64,256]{3,2,1,0:T(8,128)(2,1)S(1)} %get-tuple-element.12), channel_id=1, source_target_pairs={{0,1},{1,2},{2,3},{3,4},{4,5},{5,6},{6,7},{7,8},{8,9},{9,10},{10,1... | collective-permute-start | bytes 393224 | tf_op jit(solution)/shard_map/ppermute | solution.py:13
  65.0 100.6 %collective-permute-start.10 = (bf16[4,1,64,256]{3,2,1,0:T(8,128)(2,1)S(1)}, bf16[4,1,64,256]{3,2,1,0:T(8,128)(2,1)S(1)}, u32[]{:S(2)}, u32[]{:S(2)}) collective-permute-start(bf16[4,1,64,256]{3,2,1,0:T(8,128)(2,1)S(1)} %get-tuple-element.13), channel_id=1, source_target_pairs={{1,0},{2,1},{3,2},{4,3},{5,4},{6,5},{7,6},{8,7},{9,8},{10,9},{11,1... | collective-permute-start | bytes 393224 | tf_op jit(solution)/shard_map/ppermute | solution.py:16
  159.0 9.4 %collective-permute-start.5 = (bf16[2,6,64,256]{3,2,1,0:T(8,128)(2,1)S(1)}, bf16[2,6,64,256]{3,2,1,0:T(8,128)(2,1)S(1)}, u32[]{:S(2)}, u32[]{:S(2)}) collective-permute-start(bf16[2,6,64,256]{3,2,1,0:T(8,128)(2,1)S(1)} %pad_maximum_fusion.7), channel_id=1, source_target_pairs={{0,32},{32,64},{64,96},{1,33},{33,65},{65,97},{2,34},{34,66},{66,9... | collective-permute-start | bytes 1179656 | tf_op jit(solution)/shard_map/ppermute | solution.py:24
  166.4 13.9 %collective-permute-start.11 = (bf16[2,6,64,256]{3,2,1,0:T(8,128)(2,1)}, bf16[2,6,64,256]{3,2,1,0:T(8,128)(2,1)S(1)}, u32[]{:S(2)}, u32[]{:S(2)}) collective-permute-start(bf16[2,6,64,256]{3,2,1,0:T(8,128)(2,1)} %pad_maximum_fusion.5), channel_id=1, source_target_pairs={{32,0},{64,32},{96,64},{33,1},{65,33},{97,65},{34,2},{66,34},{98,6... | collective-permute-start | bytes 1179656 | tf_op jit(solution)/shard_map/ppermute | solution.py:24
  168.9 1.9 copy-start.2
  170.9 3.0 copy-start
  182.6 2.9 copy-start.1
  186.5 8.4 %slice-start = ((s8[7077888]{0:T(1024)(128)(4,1)}), s8[2883584]{0:T(1024)(128)(4,1)S(1)}, s32[]{:S(2)}) async-start(s8[7077888]{0:T(1024)(128)(4,1)} %bitcast.187), calls=%async_computation.1 | async-start | bytes 5767168
  186.5 3.9 %copy-start.4 = (bf16[4,4,64,256]{3,2,1,0:T(8,128)(2,1)S(1)}, bf16[4,4,64,256]{3,2,1,0:T(8,128)(2,1)}, u32[]{:S(2)}) copy-start(bf16[4,4,64,256]{3,2,1,0:T(8,128)(2,1)} %param.5) | copy-start | bytes 1572868
  186.5 8.4 %copy-start.7 = (bf16[1,3,3,64,64]{4,3,2,1,0:T(8,128)(2,1)S(1)}, bf16[1,3,3,64,64]{4,3,2,1,0:T(8,128)(2,1)}, u32[]{:S(2)}) copy-start(bf16[1,3,3,64,64]{4,3,2,1,0:T(8,128)(2,1)} %get-tuple-element.25) | copy-start | bytes 221188
  186.6 8.4 %slice-start.1 = ((s8[7077888]{0:T(1024)(128)(4,1)}), s8[4194304]{0:T(1024)(128)(4,1)S(1)}, s32[]{:S(2)}) async-start(s8[7077888]{0:T(1024)(128)(4,1)} %bitcast.187), calls=%async_computation.2 | async-start | bytes 8388608
  190.4 5.6 %copy-start.6 = (bf16[1,3,3,64,64]{4,3,2,1,0:T(8,128)(2,1)S(1)}, bf16[1,3,3,64,64]{4,3,2,1,0:T(8,128)(2,1)}, u32[]{:S(2)}) copy-start(bf16[1,3,3,64,64]{4,3,2,1,0:T(8,128)(2,1)} %get-tuple-element.24) | copy-start | bytes 221188
  194.9 2.2 copy-start.5
Sparse Core Ops, SparseCore 0:
  186.7 147.6 all-reduce.6
where the time goes:
time: 346 us; the launch traced here: 345 us
  waiting for transfers between devices  138 us (40%)
  blocking collectives  92.7 us (27%)
  starting transfers between devices  34.2 us (10%)
  matrix products  33.7 us (10%)
  local copies, waits for them, and re-layouts  25 us (7%)
  between operations  14.8 us (4%)
  other arithmetic  6.87 us (2%)
    psum x1, waiting for transfers between devices, per_device(): lax.psum((term_first, term_second, term_bias), ('frames', 'rows'))  135 us
    psum x1, blocking collectives, per_device(): lax.psum((term_first, term_second, term_bias), ('frames', 'rows'))  92.7 us
    dot_general x6, matrix products, forward_conv(): jnp.einsum('ok,frkw->frow', flat_kernel, taps[t:t + frame_count], preferr...  16.1 us
    ppermute x4, starting transfers between devices, with_halo(): lax.ppermute(lax.slice_in_dim(block, block.shape[dim] - width, None, axis...  15 us
    unnamed x58, local copies, waits for them, and re-layouts  14.3 us
    ppermute x4, starting transfers between devices, passed_along(): return lax.ppermute(value, axis, pairs)  13.9 us
    dot_general x6, matrix products, kernel_grad(): jnp.einsum('frow,frkw->ok', upstream, taps[t:t + frame_count], preferred_...  10 us
    dot_general x6, matrix products, adjoint_conv(): jnp.einsum('ck,frkw->frcw', flat_kernel, taps[2 - t:2 - t + frame_count],...  7.64 us
  transfers between devices with their start and end apart: 13, of which 2 were waited for; matrix products, arithmetic and copies ran while one was open for 12% of the time, Pallas kernels for 0%

commit v1 on v0

--- a/solution.py
+++ b/solution.py
@@ -123,7 +123,7 @@
     term_first = kernel_grad(grad_pre, input_ext)
     term_bias = jnp.sum(grad_pre.astype(jnp.float32), axis=(0, 1, 3))
     total_first, total_second, total_bias = lax.psum(
-        (term_first, term_second, term_bias), ("frames", "rows")
+        lax.psum((term_first, term_second, term_bias), "rows"), "frames"
     )
     cell_total = (
         frame_count * lax.axis_size("frames") * row_count * lax.axis_size("rows") * col_count

time: 346 us -> 637 us (1.84)
  waiting for transfers between devices: 138 us -> 415 us
  blocking collectives: 92.7 us -> 99.2 us
    psum x1 -> x2, waiting for transfers between devices: 135 us -> 410 us  [the longest x1 342 us: per_device(): lax.psum((term_first, term_second, term_bias), 'rows')]
    psum x1 -> x2, blocking collectives: 92.7 us -> 99.2 us  [the longest x1 81.1 us: per_device(): lax.psum((term_first, term_second, term_bias), 'rows')]
    unnamed x58 -> x68, local copies, waits for them, and re-layouts: 14.3 us -> 15.7 us
  transfers between devices with their start and end apart: 13 -> 14, of which waited for: 2 -> 4; matrix products, arithmetic and copies ran while one was open for 12% -> 7% of each run, Pallas kernels for 0% -> 0%
where the time goes in v1:
time: 637 us
  waiting for transfers between devices  415 us (65%)
  blocking collectives  99.2 us (16%)
  matrix products  38.7 us (6%)
  starting transfers between devices  35.3 us (6%)
  local copies, waits for them, and re-layouts  27.1 us (4%)
  between operations  14.9 us (2%)
  other arithmetic  6.78 us (1%)
    psum x1, waiting for transfers between devices, per_device(): lax.psum((term_first, term_second, term_bias), 'rows')  342 us
    psum x1, blocking collectives, per_device(): lax.psum((term_first, term_second, term_bias), 'rows')  81.1 us
    psum x1, waiting for transfers between devices, per_device(): lax.psum(lax.psum((term_first, term_second, term_bias), 'rows'), 'frames')  67.5 us
    psum x1, blocking collectives, per_device(): lax.psum(lax.psum((term_first, term_second, term_bias), 'rows'), 'frames')  18 us
    ppermute x4, starting transfers between devices, with_halo(): lax.ppermute(lax.slice_in_dim(block, block.shape[dim] - width, None, axis...  16.8 us
    unnamed x68, local copies, waits for them, and re-layouts  15.7 us
    dot_general x6, matrix products, kernel_grad(): jnp.einsum('frow,frkw->ok', upstream, taps[t:t + frame_count], preferred_...  13.1 us
    dot_general x6, matrix products, forward_conv(): jnp.einsum('ok,frkw->frow', flat_kernel, taps[t:t + frame_count], preferr...  13.1 us
  transfers between devices with their start and end apart: 14, of which 4 were waited for; matrix products, arithmetic and copies ran while one was open for 7% of the time, Pallas kernels for 0%

profile of v1, /device:TPU:1, one launch (start us, length us, event | category | flops | bytes accessed | tf_op | source)
XLA Modules:
  0.0 636.7 jit_solution(13421554620196834452)
XLA Ops:
  7.2 1.0 fusion.59
  8.3 3.9 collective-permute-start
  12.2 1.3 collective-permute-start.1
  13.5 1.7 fusion.57
  15.2 4.6 collective-permute-start.6
  19.8 1.3 collective-permute-start.7
  21.1 2.0 fusion.60
  23.2 1.1 constant_dynamic-update-slice_fusion.1
  24.3 4.9 collective-permute-start.2
  29.3 2.0 fusion.61
  35.1 1.9 collective-permute-start.8
  39.3 1.0 fusion.62
  40.4 1.0 fusion.63
  41.5 2.7 collective-permute-done.8
  46.5 1.0 fusion.65
  47.5 1.0 fusion.66
  48.6 1.3 multiply_convert_fusion
  49.9 1.5 convert_reduce_fusion
  51.4 2.1 fusion.4
  53.5 2.1 fusion.2
  55.6 4.3 collective-permute-start.3
  59.9 1.3 collective-permute-start.4
  61.2 2.1 fusion
  63.3 2.3 collective-permute-done.4
  66.4 3.3 collective-permute-start.5
  69.8 1.3 collective-permute-start.10
  71.1 4.0 collective-permute-start.9
  75.1 81.1 %psum.46 = f32[64]{0:T(128)S(1)} all-reduce(f32[64]{0:T(128)S(1)} %get-tuple-element.36), channel_id=1, replica_groups=mesh['frames'=4,'rows'=32] {'rows'}, use_global_device_ids=true, to_apply=%region_5.6 | all-reduce | flops 64 | bytes 512 | tf_op jit(solution)/shard_map/psum | solution.py:126
  156.2 18.0 %psum.47 = f32[64]{0:T(128)S(1)} all-reduce(f32[64]{0:T(128)S(1)} %psum.46), channel_id=1, replica_groups=mesh['frames'=4,'rows'=32] {'frames'}, use_global_device_ids=true, to_apply=%region_6.7 | all-reduce | flops 64 | bytes 512 | tf_op jit(solution)/shard_map/psum | solution.py:125
  175.6 2.8 collective-permute-start.11
  180.7 1.5 convolution_bitcast_fusion.2
  182.2 1.4 copy-done
  183.6 1.5 convolution_bitcast_fusion.1
  185.4 3.8 convolution_bitcast_fusion
  191.8 2.9 copy-done.1
  194.7 1.3 pad_maximum_fusion.3
  196.4 3.5 fusion.67
  200.0 3.5 convolution_add_fusion.1
  203.5 2.1 fusion.64
  205.6 1.9 fusion.17
  207.6 342.1 %all-reduce.9.cloned.1.call-done = (f32[3,3,3,64,64]{3,4,2,1,0:T(8,128)}, f32[3,3,3,64,64]{3,4,2,1,0:T(8,128)}) async-done(((f32[3,3,3,64,64]{3,4,2,1,0:T(8,128)}, f32[3,3,3,64,64]{3,4,2,1,0:T(8,128)}), (f32[3,3,3,64,64]{3,4,2,1,0:T(8,128)}, f32[3,3,3,64,64]{3,4,2,1,0:T(8,128)})) %all-reduce.9.cloned.1.call-update) | async-done | bytes 884752 | tf_op jit(solution)/shard_map/psum | solution.py:126
  549.7 3.4 convolution_add_fusion.4
  553.1 4.3 fusion.19
  557.4 67.5 %all-reduce.11.cloned.1.call-done = (f32[3,3,3,64,64]{3,4,2,1,0:T(8,128)}, f32[3,3,3,64,64]{3,4,2,1,0:T(8,128)}) async-done(((f32[3,3,3,64,64]{3,4,2,1,0:T(8,128)}, f32[3,3,3,64,64]{3,4,2,1,0:T(8,128)}), (f32[3,3,3,64,64]{3,4,2,1,0:T(8,128)}, f32[3,3,3,64,64]{3,4,2,1,0:T(8,128)})) %all-reduce.11.cloned.1.call-update) | async-done | bytes 884752 | tf_op jit(solution)/shard_map/psum | solution.py:125
  624.9 1.2 broadcast_multiply_fusion.1
  626.2 1.2 copy.52
  627.4 1.2 broadcast_multiply_fusion
  628.6 1.2 copy.53
  (111 shorter events, 15.9 us)
Async XLA Ops:
  7.2 27.8 %copy-start.2 = (bf16[4,4,64,256]{3,2,1,0:T(8,128)(2,1)S(1)}, bf16[4,4,64,256]{3,2,1,0:T(8,128)(2,1)}, u32[]{:S(2)}) copy-start(bf16[4,4,64,256]{3,2,1,0:T(8,128)(2,1)} %param.9) | copy-start | bytes 1572868
  7.2 542.5 %all-reduce.9.cloned.1.call-start = ((), (), s32[]{:S(2)}) async-start(), calls=%async_computation | async-start | bytes 3538944 | tf_op jit(solution)/shard_map/psum | solution.py:126
  8.3 14.9 %collective-permute-start = (bf16[4,1,64,256]{3,2,1,0:T(8,128)(2,1)S(1)}, bf16[4,1,64,256]{3,2,1,0:T(8,128)(2,1)S(1)}, u32[]{:S(2)}, u32[]{:S(2)}) collective-permute-start(bf16[4,1,64,256]{3,2,1,0:T(8,128)(2,1)S(1)} %get-tuple-element.21), channel_id=1, source_target_pairs={{0,1},{1,2},{2,3},{3,4},{4,5},{5,6},{6,7},{7,8},{8,9},{9,10},{10,1... | collective-permute-start | bytes 393224 | tf_op jit(solution)/shard_map/ppermute | solution.py:13
  12.2 12.0 %collective-permute-start.1 = (bf16[4,1,64,256]{3,2,1,0:T(8,128)(2,1)S(1)}, bf16[4,1,64,256]{3,2,1,0:T(8,128)(2,1)S(1)}, u32[]{:S(2)}, u32[]{:S(2)}) collective-permute-start(bf16[4,1,64,256]{3,2,1,0:T(8,128)(2,1)S(1)} %get-tuple-element.20), channel_id=1, source_target_pairs={{1,0},{2,1},{3,2},{4,3},{5,4},{6,5},{7,6},{8,7},{9,8},{10,9},{11,1... | collective-permute-start | bytes 393224 | tf_op jit(solution)/shard_map/ppermute | solution.py:16
  15.2 18.9 %collective-permute-start.6 = (bf16[4,1,64,256]{3,2,1,0:T(8,128)(2,1)}, bf16[4,1,64,256]{3,2,1,0:T(8,128)(2,1)}, u32[]{:S(2)}, u32[]{:S(2)}) collective-permute-start(bf16[4,1,64,256]{3,2,1,0:T(8,128)(2,1)} %get-tuple-element.17), channel_id=1, source_target_pairs={{0,1},{1,2},{2,3},{3,4},{4,5},{5,6},{6,7},{7,8},{8,9},{9,10},{10,1... | collective-permute-start | bytes 393224 | tf_op jit(solution)/shard_map/ppermute | solution.py:13
  19.8 15.2 %collective-permute-start.7 = (bf16[4,1,64,256]{3,2,1,0:T(8,128)(2,1)}, bf16[4,1,64,256]{3,2,1,0:T(8,128)(2,1)S(1)}, u32[]{:S(2)}, u32[]{:S(2)}) collective-permute-start(bf16[4,1,64,256]{3,2,1,0:T(8,128)(2,1)} %get-tuple-element.16), channel_id=1, source_target_pairs={{1,0},{2,1},{3,2},{4,3},{5,4},{6,5},{7,6},{8,7},{9,8},{10,9},{11,1... | collective-permute-start | bytes 393224 | tf_op jit(solution)/shard_map/ppermute | solution.py:16
  24.3 12.7 %collective-permute-start.2 = (bf16[2,6,64,256]{3,2,1,0:T(8,128)(2,1)S(1)}, bf16[2,6,64,256]{3,2,1,0:T(8,128)(2,1)S(1)}, u32[]{:S(2)}, u32[]{:S(2)}) collective-permute-start(bf16[2,6,64,256]{3,2,1,0:T(8,128)(2,1)S(1)} %slice.306), channel_id=1, source_target_pairs={{0,32},{32,64},{64,96},{1,33},{33,65},{65,97},{2,34},{34,66},{66,9... | collective-permute-start | bytes 1179656 | tf_op jit(solution)/shard_map/ppermute | solution.py:24
  35.1 9.1 %collective-permute-start.8 = (bf16[2,6,64,256]{3,2,1,0:T(8,128)(2,1)S(1)}, bf16[2,6,64,256]{3,2,1,0:T(8,128)(2,1)S(1)}, u32[]{:S(2)}, u32[]{:S(2)}) collective-permute-start(bf16[2,6,64,256]{3,2,1,0:T(8,128)(2,1)S(1)} %slice.318), channel_id=1, source_target_pairs={{32,0},{64,32},{96,64},{33,1},{65,33},{97,65},{34,2},{66,34},{98,6... | collective-permute-start | bytes 1179656 | tf_op jit(solution)/shard_map/ppermute | solution.py:24
  38.3 2.1 copy-start.7
  46.1 2.5 copy-start.13
  47.5 2.4 copy-start.12
  55.6 7.7 %collective-permute-start.3 = (bf16[4,1,64,256]{3,2,1,0:T(8,128)(2,1)S(1)}, bf16[4,1,64,256]{3,2,1,0:T(8,128)(2,1)S(1)}, u32[]{:S(2)}, u32[]{:S(2)}) collective-permute-start(bf16[4,1,64,256]{3,2,1,0:T(8,128)(2,1)S(1)} %get-tuple-element.18), channel_id=1, source_target_pairs={{0,1},{1,2},{2,3},{3,4},{4,5},{5,6},{6,7},{7,8},{8,9},{9,10},{10,1... | collective-permute-start | bytes 393224 | tf_op jit(solution)/shard_map/ppermute | solution.py:13
  59.9 5.7 collective-permute-start.4
  66.4 112.0 %collective-permute-start.5 = (bf16[2,6,64,256]{3,2,1,0:T(8,128)(2,1)}, bf16[2,6,64,256]{3,2,1,0:T(8,128)(2,1)S(1)}, u32[]{:S(2)}, u32[]{:S(2)}) collective-permute-start(bf16[2,6,64,256]{3,2,1,0:T(8,128)(2,1)} %pad_maximum_fusion.7), channel_id=1, source_target_pairs={{0,32},{32,64},{64,96},{1,33},{33,65},{65,97},{2,34},{34,66},{66,9... | collective-permute-start | bytes 1179656 | tf_op jit(solution)/shard_map/ppermute | solution.py:24
  69.8 105.0 %collective-permute-start.10 = (bf16[4,1,64,256]{3,2,1,0:T(8,128)(2,1)S(1)}, bf16[4,1,64,256]{3,2,1,0:T(8,128)(2,1)S(1)}, u32[]{:S(2)}, u32[]{:S(2)}) collective-permute-start(bf16[4,1,64,256]{3,2,1,0:T(8,128)(2,1)S(1)} %get-tuple-element.15), channel_id=1, source_target_pairs={{1,0},{2,1},{3,2},{4,3},{5,4},{6,5},{7,6},{8,7},{9,8},{10,9},{11,1... | collective-permute-start | bytes 393224 | tf_op jit(solution)/shard_map/ppermute | solution.py:16
  71.1 103.7 %collective-permute-start.9 = (bf16[4,1,64,256]{3,2,1,0:T(8,128)(2,1)S(1)}, bf16[4,1,64,256]{3,2,1,0:T(8,128)(2,1)S(1)}, u32[]{:S(2)}, u32[]{:S(2)}) collective-permute-start(bf16[4,1,64,256]{3,2,1,0:T(8,128)(2,1)S(1)} %get-tuple-element.14), channel_id=1, source_target_pairs={{0,1},{1,2},{2,3},{3,4},{4,5},{5,6},{6,7},{7,8},{8,9},{9,10},{10,1... | collective-permute-start | bytes 393224 | tf_op jit(solution)/shard_map/ppermute | solution.py:13
  175.6 13.8 %collective-permute-start.11 = (bf16[2,6,64,256]{3,2,1,0:T(8,128)(2,1)}, bf16[2,6,64,256]{3,2,1,0:T(8,128)(2,1)S(1)}, u32[]{:S(2)}, u32[]{:S(2)}) collective-permute-start(bf16[2,6,64,256]{3,2,1,0:T(8,128)(2,1)} %pad_maximum_fusion.5), channel_id=1, source_target_pairs={{32,0},{64,32},{96,64},{33,1},{65,33},{97,65},{34,2},{66,34},{98,6... | collective-permute-start | bytes 1179656 | tf_op jit(solution)/shard_map/ppermute | solution.py:24
  180.7 2.9 copy-start
  189.9 4.9 copy-start.9
  189.9 4.8 copy-start.10
  189.9 4.8 copy-start.11
  191.8 2.9 copy-start.1
  196.1 7.4 %slice-start = ((s8[7077888]{0:T(1024)(128)(4,1)}), s8[2883584]{0:T(1024)(128)(4,1)S(1)}, s32[]{:S(2)}) async-start(s8[7077888]{0:T(1024)(128)(4,1)} %bitcast.187), calls=%async_computation.2 | async-start | bytes 5767168
  196.1 428.8 %all-reduce.11.cloned.1.call-start = ((), (), s32[]{:S(2)}) async-start(), calls=%async_computation.1 | async-start | bytes 3538944 | tf_op jit(solution)/shard_map/psum | solution.py:125
  196.4 7.2 %copy-start.6 = (bf16[64,3,3,64]{0,3,2,1:T(8,128)(2,1)S(1)}, bf16[64,3,3,64]{0,3,2,1:T(8,128)(2,1)}, u32[]{:S(2)}) copy-start(bf16[64,3,3,64]{0,3,2,1:T(8,128)(2,1)} %copy.36) | copy-start | bytes 221188
  196.4 7.2 %slice-start.1 = ((s8[7077888]{0:T(1024)(128)(4,1)}), s8[4194304]{0:T(1024)(128)(4,1)S(1)}, s32[]{:S(2)}) async-start(s8[7077888]{0:T(1024)(128)(4,1)} %bitcast.187), calls=%async_computation.3 | async-start | bytes 8388608
  199.9 5.7 slice-start.2
  199.9 5.7 copy-start.8
  199.9 5.7 slice-start.3
  205.6 344.1 %copy-start.3 = (f32[4,4,256,64]{2,3,1,0:T(8,128)S(1)}, f32[4,4,256,64]{2,3,1,0:T(8,128)}, u32[]{:S(2)}) copy-start(f32[4,4,256,64]{2,3,1,0:T(8,128)} %fusion.64) | copy-start | bytes 3145732
  205.6 344.1 %copy-start.5 = (bf16[64,3,3,64]{0,3,2,1:T(8,128)(2,1)S(1)}, bf16[64,3,3,64]{0,3,2,1:T(8,128)(2,1)}, u32[]{:S(2)}) copy-start(bf16[64,3,3,64]{0,3,2,1:T(8,128)(2,1)} %copy.34) | copy-start | bytes 221188
  205.6 347.5 %copy-start.4 = (bf16[4,4,64,256]{3,2,1,0:T(8,128)(2,1)S(1)}, bf16[4,4,64,256]{3,2,1,0:T(8,128)(2,1)}, u32[]{:S(2)}) copy-start(bf16[4,4,64,256]{3,2,1,0:T(8,128)(2,1)} %param.5) | copy-start | bytes 1572868
Sparse Core Ops, SparseCore 0:
  196.2 353.4 all-reduce.8
  552.2 72.6 all-reduce.10
